TPU v7x, 256 devices: a whole 4x4x8 slice. The times are simulated.
256 devices in a mesh: bins: 16 (over y, z_hi, core), batch: 16 (over x, z_lo).
Axes of the slice: x: 4, y: 4, z: 8 (z_hi: 2, z_lo: 4; z = z_hi * 4 + z_lo), core: 2. Of those that a mesh axis runs over, the one named last changes fastest.
Arguments:
- features: bfloat16 [16, 4096, 1536], P('batch', 'bins'), may hold values from -6 to 6
- norm_gain: float32 [1536], replicated, may hold values from 0.25 to 1.75
- convolution_taps_weight: bfloat16 [3, 1536, 768], replicated, may hold values from -0.09375 to 0.09375
- out_weight: bfloat16 [768, 1536], replicated, may hold values from -0.21875 to 0.21875
- head_weight: bfloat16 [1536, 4096], P(None, 'batch'), may hold values from -0.15625 to 0.15625
- rc_perm: int32 [1536], replicated, may hold values from 0 to 1535, each once
- exon_bins: int32 [16, 64, 8], P('batch'), may hold values from 0 to 4095, as said below
- exon_count: int32 [16, 64], P('batch'), may hold values from 1 to 8
- gene_strand: int32 [16, 64], P('batch'), may hold values 0 or 1
- gene_target: float32 [16, 64, 4096], P('batch', 'bins'), may hold values from 0.5 to 8
Outputs:
- input_grad: bfloat16 [16, 4096, 1536], P('batch', 'bins')
- out_weight_grad: float32 [768, 1536], P('batch')
Inputs may be any that keep to these rules, and one draw needn't show every extreme that they name: `rc_perm`: a permutation of the channels. `exon_bins`: bins of the gene's own sequence; a bin may be listed more than once; each gene's listed bins lie within 256 consecutive bins. All genes of a sequence may lie within the same 256 bins j * 256 to (j + 1) * 256 - 1 of one j, and then every one of those bins may be listed and counted.
All inputs are finite; a program needn't handle non-finite values. No bound on the sum of `gene_strand` on one device may be relied on, other than what follows from the above.
Results may differ from a plain program's by a relative error of at most 0.014.
Values may be sent and summed in bfloat16 or wider, within the bound.
No kernel may reach another device: no remote copies, remote signals or barrier semaphores. Data moves between devices by JAX's collectives and lax.ppermute only.
A program may use at most 128 MiB of HBM per device.

v0:
```python
import jax
import jax.numpy as jnp
from jax import lax
from jax.sharding import PartitionSpec as P

DILATION_STEP = 16


def with_halo(block, sides, width):
    for axis, dim in sides:
        count = lax.axis_size(axis)
        forward = [(i, i + 1) for i in range(count - 1)]
        backward = [(target, source) for source, target in forward]
        low = lax.ppermute(
            lax.slice_in_dim(block, block.shape[dim] - width, None, axis=dim), axis, forward
        )
        high = lax.ppermute(lax.slice_in_dim(block, 0, width, axis=dim), axis, backward)
        block = jnp.concatenate([low, block, high], axis=dim)
    return block


def gelu_slope(argument):
    return (
        0.5 * (1.0 + jax.scipy.special.erf(argument * 0.7071067811865476))
        + argument * jnp.exp(-0.5 * argument * argument) * 0.3989422804014327
    )


def pair_flip(matrix, strand):
    swapped = matrix.reshape(matrix.shape[0], -1, 2)[:, :, ::-1].reshape(matrix.shape)
    return jnp.where(strand[:, None] == 1, swapped, matrix)


def exon_hits(bin_lists, counts, positions):
    listed = jnp.arange(bin_lists.shape[1], dtype=jnp.int32)[None, :] < counts[:, None]
    matched = (bin_lists[:, :, None] == positions[None, None, :]) & listed[:, :, None]
    return jnp.sum(matched.astype(jnp.float32), axis=1).astype(jnp.bfloat16)


def per_device(
    features,
    norm_gain,
    convolution_taps_weight,
    out_weight,
    head_weight,
    rc_perm,
    exon_bins,
    exon_count,
    gene_strand,
    gene_target,
):
    bin_devices = lax.axis_size("bins")
    bin_index = lax.axis_index("bins")
    widened = features[0].astype(jnp.float32)
    count_of_rows = widened.shape[0]
    channels = widened.shape[1]
    inverse = lax.rsqrt(jnp.mean(widened * widened, axis=-1, keepdims=True) + 1e-06)
    normed = widened * inverse * norm_gain
    hidden_state = jax.nn.gelu(normed, approximate=False).astype(jnp.bfloat16)
    padded_input = with_halo(hidden_state, (("bins", 0),), DILATION_STEP)
    convolved_sum = jnp.zeros((count_of_rows, convolution_taps_weight.shape[2]), jnp.float32)
    for kernel_tap_index in range(3):
        convolved_sum = convolved_sum + jnp.dot(
            padded_input[
                kernel_tap_index * DILATION_STEP : kernel_tap_index * DILATION_STEP + count_of_rows
            ],
            convolution_taps_weight[kernel_tap_index],
            preferred_element_type=jnp.float32,
        )
    active = jax.nn.gelu(convolved_sum, approximate=False).astype(jnp.bfloat16)
    block_out = (widened + jnp.dot(active, out_weight, preferred_element_type=jnp.float32)).astype(
        jnp.bfloat16
    )
    whole_head = lax.all_gather(head_weight, "batch", axis=1, tiled=True)
    logits = jnp.dot(block_out, whole_head, preferred_element_type=jnp.float32)
    predicted = jax.nn.softplus(logits).astype(jnp.bfloat16)
    positions = bin_index * count_of_rows + jnp.arange(count_of_rows, dtype=jnp.int32)
    hit_counts = exon_hits(exon_bins[0], exon_count[0], positions)
    partial_value = jnp.dot(hit_counts, predicted, preferred_element_type=jnp.float32)
    own_genes = gene_target.shape[1]
    owned_sum = lax.psum_scatter(
        partial_value.astype(jnp.bfloat16), "bins", scatter_dimension=0, tiled=True
    ).astype(jnp.float32)
    own_strand = lax.dynamic_slice_in_dim(gene_strand[0], bin_index * own_genes, own_genes, 0)
    coverage = pair_flip(owned_sum, own_strand)
    adjoint = (1.0 - gene_target[0] / (1.0 + coverage)).astype(jnp.bfloat16)
    spread_back = lax.all_gather(pair_flip(adjoint, own_strand), "bins", axis=0, tiled=True)
    pred_grad = lax.dot_general(
        hit_counts, spread_back, (((0,), (0,)), ((), ())), preferred_element_type=jnp.float32
    )
    logit_grad = (pred_grad * jax.nn.sigmoid(logits)).astype(jnp.bfloat16)
    head_back = lax.dot_general(
        logit_grad, whole_head, (((1,), (1,)), ((), ())), preferred_element_type=jnp.float32
    )
    pieces = block_out.reshape(bin_devices, count_of_rows // bin_devices, channels)
    outbound = lax.all_to_all(pieces, "bins", split_axis=0, concat_axis=0, tiled=True)
    returned = lax.all_to_all(outbound[::-1], "bins", split_axis=0, concat_axis=0, tiled=True)
    partner = returned.reshape(count_of_rows, channels)
    mirrored = partner[::-1].astype(jnp.float32)
    inverse_perm = (
        jnp.zeros((channels,), jnp.int32).at[rc_perm].set(jnp.arange(channels, dtype=jnp.int32))
    )
    block_wide = block_out.astype(jnp.float32)
    rc_grad = block_wide - 0.5 * (mirrored[:, rc_perm] + mirrored[:, inverse_perm])
    block_grad = (head_back + rc_grad).astype(jnp.bfloat16)
    batch_share = lax.psum_scatter(
        lax.dot_general(
            active, block_grad, (((0,), (0,)), ((), ())), preferred_element_type=jnp.float32
        ).astype(jnp.bfloat16),
        "batch",
        scatter_dimension=0,
        tiled=True,
    )
    out_weight_grad = lax.psum(batch_share, "bins").astype(jnp.float32)
    activation_gradient = (
        lax.dot_general(
            block_grad, out_weight, (((1,), (1,)), ((), ())), preferred_element_type=jnp.float32
        )
        * gelu_slope(convolved_sum)
    ).astype(jnp.bfloat16)
    padded_gradient = with_halo(activation_gradient, (("bins", 0),), DILATION_STEP)
    hidden_grad = jnp.zeros((count_of_rows, channels), jnp.float32)
    for kernel_tap_index in range(3):
        shift_amount = (2 - kernel_tap_index) * DILATION_STEP
        hidden_grad = hidden_grad + lax.dot_general(
            padded_gradient[shift_amount : shift_amount + count_of_rows],
            convolution_taps_weight[kernel_tap_index],
            (((1,), (1,)), ((), ())),
            preferred_element_type=jnp.float32,
        )
    normed_grad = hidden_grad * gelu_slope(normed) * norm_gain
    norm_back = inverse * normed_grad - widened * inverse**3 * jnp.mean(
        normed_grad * widened, axis=-1, keepdims=True
    )
    input_grad = (block_grad.astype(jnp.float32) + norm_back).astype(jnp.bfloat16)
    return (input_grad[None], out_weight_grad)


def solution(mesh):
    in_specs = (
        P("batch", "bins", None),
        P(),
        P(),
        P(),
        P(None, "batch"),
        P(),
        P("batch", None, None),
        P("batch", None),
        P("batch", None),
        P("batch", "bins", None),
    )
    out_specs = (P("batch", "bins", None), P("batch", None))
    return jax.shard_map(
        per_device, mesh=mesh, in_specs=in_specs, out_specs=out_specs, check_vma=False
    )
```

profile of v0, /device:TPU:1, one launch (start us, length us, event | category | flops | bytes accessed | tf_op | source)
XLA Modules:
  0.0 843.6 jit_solution(11148175389871781188)
XLA Ops:
  7.2 0.7 all-gather.3.cloned.1.call-update
  7.9 1.4 fusion.32
  9.4 3.8 fusion.39
  13.2 5.1 collective-permute-start.1
  18.3 7.3 collective-permute-start
  25.6 5.9 fusion.13
  31.5 0.8 fusion.9
  32.3 3.2 fusion.101
  35.5 1.7 fusion.6
  37.2 10.4 %all-to-all-start = ((bf16[16,16,1536]{2,1,0:T(8,128)(2,1)}), bf16[16,16,1536]{2,1,0:T(8,128)(2,1)S(1)}, u32[]{:S(2)}, u32[]{:S(2)}) async-start(bf16[16,16,1536]{2,1,0:T(8,128)(2,1)} %bitcast.188), calls=%async_computation | async-start | bytes 1572864 | tf_op jit(solution)/shard_map/all_to_all | solution.py:96
  47.8 2.0 copy.32
  51.0 6.4 scatter_custom_fusion
  57.8 18.2 %all-to-all-done = bf16[16,16,1536]{2,1,0:T(8,128)(2,1)S(1)} async-done(((bf16[16,16,1536]{2,1,0:T(8,128)(2,1)}), bf16[16,16,1536]{2,1,0:T(8,128)(2,1)S(1)}, u32[]{:S(2)}, u32[]{:S(2)}) %all-to-all-start) | async-done | bytes 786464 | tf_op jit(solution)/shard_map/all_to_all | solution.py:96
  76.0 0.9 rev.14
  77.0 4.0 all-to-all-start.1
  81.1 235.8 %all-gather.3.cloned.1.call-done = bf16[1536,4096]{1,0:T(8,128)(2,1)} async-done(((bf16[1536,256]{1,0:T(8,128)(2,1)}), bf16[1536,4096]{1,0:T(8,128)(2,1)}) %all-gather.3.cloned.1.call-update) | async-done | bytes 12582928 | tf_op jit(solution)/shard_map/all_gather | solution.py:74
  316.9 6.6 fusion.195
  323.6 1.9 copy-done.15
  325.5 3.2 convolution_convert_fusion
  329.0 1.2 copy.35
  330.1 10.3 %rev.15 = bf16[256,1536]{0,1:T(8,128)(2,1)S(1)} reverse(bf16[256,1536]{0,1:T(8,128)(2,1)} %copy.35), dimensions={0} | reverse | bytes 1572864 | tf_op jit(solution)/shard_map/rev | solution.py:99
  340.5 1.3 convert_element_type.84
  341.8 6.1 gather_fusion.1
  347.9 3.0 copy.37
  350.9 6.1 gather_fusion
  357.0 3.1 copy.36
  360.1 148.3 %all-reduce.6.cloned.1.call-done = bf16[64,4096]{1,0:T(8,128)(2,1)} async-done(((bf16[64,4096]{1,0:T(8,128)(2,1)}), bf16[64,4096]{1,0:T(8,128)(2,1)}) %all-reduce.6.cloned.1.call-update) | async-done | bytes 524304
  508.4 0.9 constant_dynamic-slice_fusion
  509.7 7.8 rev.12
  517.5 3.7 fusion.19
  521.2 10.2 %rev.13 = bf16[4,2048,2]{0,2,1:T(2,128)(2,1)} reverse(bf16[4,2048,2]{0,2,1:T(2,128)(2,1)} %bitcast.184), dimensions={2} | reverse | bytes 65536 | tf_op jit(solution)/shard_map/rev | solution.py:30
  531.4 2.3 select_bitcast_fusion
  533.7 1.6 copy.34
  535.3 31.2 %all-gather = bf16[16,4,4096]{2,1,0:T(4,128)(2,1)S(1)} all-gather(bf16[1,4,4096]{2,1,0:T(4,128)(2,1)S(1)} %copy.34), channel_id=1, replica_groups=mesh['bins'=16,'batch'=16] {'bins'}, dimensions={0}, use_global_device_ids=true | all-gather | bytes 557056 | tf_op jit(solution)/shard_map/all_gather | solution.py:87
  566.5 0.9 reshape.131
  567.4 10.1 %fusion.5 = bf16[256,1536]{1,0:T(8,128)(2,1)S(1)} fusion(bf16[1536,4096]{1,0:T(8,128)(2,1)} %all-gather.3.cloned.1.call-done, bf16[64,4096]{1,0:T(8,128)(2,1)} %reshape.131, f32[256,4096]{1,0:T(8,128)} %copy-done.15, f32[1536,256]{0,1:T(8,128)} %copy.36, f32[1536,256]{0,1:T(8,128)} %copy.37, bf16[256,1536]{1,0:T(8,128)(2,1)} %fusion.6, ...), kind=kOutput, calls=%fused_computation.15 | convolution fusion | flops 3363045376 | bytes 22052864 | tf_op jit(solution)/shard_map/dot_general | solution.py:92
  577.5 2.2 convolution_convert_fusion.1
  580.0 2.0 fusion.98
  582.1 2.8 collective-permute-start.3
  584.9 2.6 fusion.11
  587.5 2.1 collective-permute-start.2
  589.6 2.5 fusion.7
  592.0 5.1 collective-permute-done.2
  597.2 4.2 fusion.56
  601.4 55.1 %reduce-scatter.2.cloned.1.call-done = bf16[48,1536]{1,0:T(8,128)(2,1)} async-done(((bf16[768,1536]{1,0:T(8,128)(2,1)}), bf16[48,1536]{1,0:T(8,128)(2,1)}) %reduce-scatter.2.cloned.1.call-update) | async-done | bytes 147472 | tf_op jit(solution)/shard_map/reduce_scatter | solution.py:106
  656.5 2.9 fusion.108
  659.5 175.9 %all-reduce.4.cloned.1.call-done = bf16[48,1536]{1,0:T(8,128)(2,1)} async-done(((bf16[48,1536]{1,0:T(8,128)(2,1)}), bf16[48,1536]{1,0:T(8,128)(2,1)}) %all-reduce.4.cloned.1.call-update) | async-done | bytes 147472 | tf_op jit(solution)/shard_map/psum | solution.py:114
  835.4 1.6 convert_element_type.90
  (63 shorter events, 2.2 us)
Async XLA Ops:
  7.2 28.4 %copy-start = (bf16[768,1536]{1,0:T(8,128)(2,1)S(1)}, bf16[768,1536]{1,0:T(8,128)(2,1)}, u32[]{:S(2)}) copy-start(bf16[768,1536]{1,0:T(8,128)(2,1)} %param.13) | copy-start | bytes 7077892
  7.2 2.2 copy-start.2
  7.2 2.2 copy-start.9
  7.2 309.7 %all-gather.3.cloned.1.call-start = ((), (), s32[]{:S(2)}) async-start(), calls=%async_computation.3 | async-start | bytes 13369344 | tf_op jit(solution)/shard_map/all_gather | solution.py:74
  13.2 18.3 %collective-permute-start.1 = (bf16[16,1536]{1,0:T(8,128)(2,1)S(1)}, bf16[16,1536]{1,0:T(8,128)(2,1)S(1)}, u32[]{:S(2)}, u32[]{:S(2)}) collective-permute-start(bf16[16,1536]{1,0:T(8,128)(2,1)S(1)} %get-tuple-element.3), channel_id=1, source_target_pairs={{16,0},{32,16},{48,32},{64,48},{80,64},{96,80},{112,96},{128,112},... | collective-permute-start | bytes 147464 | tf_op jit(solution)/shard_map/ppermute | solution.py:17
  18.3 13.2 %slice-start = ((s8[7077888]{0:T(1024)(128)(4,1)}), s8[4194304]{0:T(1024)(128)(4,1)S(1)}, s32[]{:S(2)}) async-start(s8[7077888]{0:T(1024)(128)(4,1)} %bitcast.191), calls=%async_computation.7 | async-start | bytes 8388608
  18.3 13.2 %slice-start.1 = ((s8[7077888]{0:T(1024)(128)(4,1)}), s8[2883584]{0:T(1024)(128)(4,1)S(1)}, s32[]{:S(2)}) async-start(s8[7077888]{0:T(1024)(128)(4,1)} %bitcast.191), calls=%async_computation.8 | async-start | bytes 5767168
  18.3 14.0 %collective-permute-start = (bf16[16,1536]{1,0:T(8,128)(2,1)S(1)}, bf16[16,1536]{1,0:T(8,128)(2,1)S(1)}, u32[]{:S(2)}, u32[]{:S(2)}) collective-permute-start(bf16[16,1536]{1,0:T(8,128)(2,1)S(1)} %get-tuple-element.2), channel_id=1, source_target_pairs={{0,16},{16,32},{32,48},{48,64},{64,80},{80,96},{96,112},{112,128},... | collective-permute-start | bytes 147464 | tf_op jit(solution)/shard_map/ppermute | solution.py:14
  35.5 1.7 copy-start.5
  37.2 10.5 %copy-start.11 = (s32[1,64,8]{1,2,0:T(8,128)S(1)}, s32[1,64,8]{1,2,0:T(8,128)}, u32[]{:S(2)}) copy-start(s32[1,64,8]{1,2,0:T(8,128)} %param.16) | copy-start | bytes 6148
  37.2 10.6 %copy-start.7 = (f32[1,4,4096]{2,1,0:T(4,128)S(1)}, f32[1,4,4096]{2,1,0:T(4,128)}, u32[]{:S(2)}) copy-start(f32[1,4,4096]{2,1,0:T(4,128)} %param.19) | copy-start | bytes 196612
  37.2 12.6 %copy-start.14 = (u32[256]{0:T(256)S(1)}, u32[256]{0:T(256)}, u32[]{:S(2)}) copy-start(u32[256]{0:T(256)} %constant.19) | copy-start | bytes 3076
  37.2 13.8 %copy-start.10 = (s32[1536]{0:T(1024)S(1)}, s32[1536]{0:T(1024)}, u32[]{:S(2)}) copy-start(s32[1536]{0:T(1024)} %param.15) | copy-start | bytes 18436
  37.2 20.2 %copy-start.12 = (s32[1,64]{1,0:T(1,128)S(1)}, s32[1,64]{1,0:T(1,128)}, u32[]{:S(2)}) copy-start(s32[1,64]{1,0:T(1,128)} %param.17) | copy-start | bytes 772
  37.2 38.8 %all-to-all-start = ((bf16[16,16,1536]{2,1,0:T(8,128)(2,1)}), bf16[16,16,1536]{2,1,0:T(8,128)(2,1)S(1)}, u32[]{:S(2)}, u32[]{:S(2)}) async-start(bf16[16,16,1536]{2,1,0:T(8,128)(2,1)} %bitcast.188), calls=%async_computation | async-start | bytes 1572864 | tf_op jit(solution)/shard_map/all_to_all | solution.py:96
  57.8 265.8 %copy-start.8 = (bf16[64,256]{1,0:T(8,128)(2,1)}, bf16[64,256]{1,0:T(8,128)(2,1)S(1)}, u32[]{:S(2)}) copy-start(bf16[64,256]{1,0:T(8,128)(2,1)S(1)} %convert_reduce_fusion) | copy-start | bytes 98308
  77.0 252.0 %all-to-all-start.1 = ((bf16[16,16,1536]{2,1,0:T(8,128)(2,1)}), bf16[16,16,1536]{2,1,0:T(8,128)(2,1)S(1)}, u32[]{:S(2)}, u32[]{:S(2)}) async-start(bf16[16,16,1536]{2,1,0:T(8,128)(2,1)} %rev.14), calls=%async_computation.1 | async-start | bytes 1572864 | tf_op jit(solution)/shard_map/all_to_all | solution.py:97
  81.0 427.3 %all-reduce.6.cloned.1.call-start = ((), (), s32[]{:S(2)}) async-start(), calls=%async_computation.6 | async-start | bytes 1048576
  323.6 2.0 copy-start.15
  325.5 3.3 copy-start.13
  328.8 327.7 %reduce-scatter.2.cloned.1.call-start = ((), (), s32[]{:S(2)}) async-start(), calls=%async_computation.4 | async-start | bytes 2506752 | tf_op jit(solution)/shard_map/reduce_scatter | solution.py:106
  521.2 10.2 %copy-start.1 = (bf16[4,4096]{0,1:T(8,128)(2,1)S(1)}, bf16[4,4096]{0,1:T(8,128)(2,1)}, u32[]{:S(2)}) copy-start(bf16[4,4096]{0,1:T(8,128)(2,1)} %fusion.19) | copy-start | bytes 98308
  567.4 10.1 %copy-start.6 = (bf16[256,768]{1,0:T(8,128)(2,1)S(1)}, bf16[256,768]{1,0:T(8,128)(2,1)}, u32[]{:S(2)}) copy-start(bf16[256,768]{1,0:T(8,128)(2,1)} %copy-done.5) | copy-start | bytes 1179652
  577.5 2.5 copy-start.4
  579.8 255.6 %all-reduce.4.cloned.1.call-start = ((), (), s32[]{:S(2)}) async-start(), calls=%async_computation.5 | async-start | bytes 294912 | tf_op jit(solution)/shard_map/psum | solution.py:114
  582.1 7.5 collective-permute-start.3
  587.5 9.7 %copy-start.3 = (bf16[1,256,1536]{2,1,0:T(8,128)(2,1)S(1)}, bf16[1,256,1536]{2,1,0:T(8,128)(2,1)}, u32[]{:S(2)}) copy-start(bf16[1,256,1536]{2,1,0:T(8,128)(2,1)} %param.10) | copy-start | bytes 2359300
  587.5 9.7 %collective-permute-start.2 = (bf16[16,768]{1,0:T(8,128)(2,1)S(1)}, bf16[16,768]{1,0:T(8,128)(2,1)S(1)}, u32[]{:S(2)}, u32[]{:S(2)}) collective-permute-start(bf16[16,768]{1,0:T(8,128)(2,1)S(1)} %get-tuple-element.4), channel_id=1, source_target_pairs={{16,0},{32,16},{48,32},{64,48},{80,64},{96,80},{112,96},{128,112},... | collective-permute-start | bytes 73736 | tf_op jit(solution)/shard_map/ppermute | solution.py:17
Sparse Core Ops, SparseCore 0:
  9.7 307.1 all-gather.2
  328.9 179.4 all-reduce.5
  579.9 76.5 reduce-scatter.1
  659.0 176.3 all-reduce.3
where the time goes:
time: 846 us; the launch traced here: 844 us
  waiting for transfers between devices  639 us (76%)
  local copies, waits for them, and re-layouts  63.7 us (8%)
  matrix products  45 us (5%)
  starting transfers between devices  32.1 us (4%)
  blocking collectives  31.2 us (4%)
  other arithmetic  17.5 us (2%)
  between operations  14.8 us (2%)
    all_gather x1, waiting for transfers between devices, per_device(): whole_head = lax.all_gather(head_weight, 'batch', axis=1, tiled=True)  236 us
    psum x1, waiting for transfers between devices, per_device(): out_weight_grad = lax.psum(batch_share, 'bins').astype(jnp.float32)  176 us
    unnamed x5, waiting for transfers between devices  149 us
    reduce_scatter x1, waiting for transfers between devices, per_device(): lax.psum_scatter(lax.dot_general(active, block_grad, (((0,), (0,)), ((),...  55.1 us
    all_gather x1, blocking collectives, per_device(): lax.all_gather(pair_flip(adjoint, own_strand), 'bins', axis=0, tiled=True)  31.2 us
    all_to_all x1, waiting for transfers between devices, per_device(): lax.all_to_all(pieces, 'bins', split_axis=0, concat_axis=0, tiled=True)  18.2 us
    rev x2, local copies, waits for them, and re-layouts, pair_flip(): matrix.reshape(matrix.shape[0], -1, 2)[:, :, ::-1].reshape(matrix.shape)  18 us
  transfers between devices with their start and end apart: 10, of which 6 were waited for; matrix products, arithmetic and copies ran while one was open for 10% of the time, Pallas kernels for 0%

commit v1 on v0

--- a/solution.py
+++ b/solution.py
@@ -111,7 +111,7 @@
         scatter_dimension=0,
         tiled=True,
     )
-    out_weight_grad = lax.psum(batch_share, "bins").astype(jnp.float32)
+    out_weight_grad = jnp.sum(lax.all_gather(batch_share, "bins"), axis=0).astype(jnp.float32)
     activation_gradient = (
         lax.dot_general(
             block_grad, out_weight, (((1,), (1,)), ((), ())), preferred_element_type=jnp.float32

time: 846 us -> 745 us (0.88)
  waiting for transfers between devices: 639 us -> 526 us
  starting transfers between devices: 32.1 us -> 45.9 us
    psum x1 -> x0, waiting for transfers between devices: 176 us -> none  [per_device(): out_weight_grad = lax.psum(batch_share, 'bins').astype(jnp.float32)]
    all_gather x0 -> x1, waiting for transfers between devices: none -> 39.4 us  [per_device(): lax.all_gather(batch_share, 'bins')]
    reduce_scatter x1, waiting for transfers between devices: 55.1 us -> 77.4 us  [per_device(): lax.psum_scatter(lax.dot_general(active, block_grad, (((0,), (0,)), ((),...]
    ppermute x2, starting transfers between devices: 10.1 us -> 23.9 us  [with_halo(): lax.ppermute(lax.slice_in_dim(block, block.shape[dim] - width, None, axis...]
  transfers between devices with their start and end apart: 10 -> 10, of which waited for: 6 -> 6; matrix products, arithmetic and copies ran while one was open for 10% -> 11% of each run, Pallas kernels for 0% -> 0%
where the time goes in v1:
time: 745 us; the launch traced here: 742 us
  waiting for transfers between devices  526 us (71%)
  local copies, waits for them, and re-layouts  63.9 us (9%)
  starting transfers between devices  45.9 us (6%)
  matrix products  43.8 us (6%)
  blocking collectives  31.2 us (4%)
  other arithmetic  17.1 us (2%)
  between operations  14.8 us (2%)
    all_gather x1, waiting for transfers between devices, per_device(): whole_head = lax.all_gather(head_weight, 'batch', axis=1, tiled=True)  236 us
    unnamed x5, waiting for transfers between devices  149 us
    reduce_scatter x1, waiting for transfers between devices, per_device(): lax.psum_scatter(lax.dot_general(active, block_grad, (((0,), (0,)), ((),...  77.4 us
    all_gather x1, waiting for transfers between devices, per_device(): lax.all_gather(batch_share, 'bins')  39.4 us
    all_gather x1, blocking collectives, per_device(): lax.all_gather(pair_flip(adjoint, own_strand), 'bins', axis=0, tiled=True)  31.2 us
    ppermute x2, starting transfers between devices, with_halo(): lax.ppermute(lax.slice_in_dim(block, block.shape[dim] - width, None, axis...  23.9 us
    all_to_all x1, waiting for transfers between devices, per_device(): lax.all_to_all(pieces, 'bins', split_axis=0, concat_axis=0, tiled=True)  18.2 us
    rev x2, local copies, waits for them, and re-layouts, pair_flip(): matrix.reshape(matrix.shape[0], -1, 2)[:, :, ::-1].reshape(matrix.shape)  18.1 us
  transfers between devices with their start and end apart: 10, of which 6 were waited for; matrix products, arithmetic and copies ran while one was open for 11% of the time, Pallas kernels for 0%

profile of v1, /device:TPU:1, one launch (start us, length us, event | category | flops | bytes accessed | tf_op | source)
XLA Modules:
  0.0 742.2 jit_solution(1971589088693684619)
XLA Ops:
  7.9 1.4 fusion.32
  9.4 3.8 fusion.39
  13.2 5.1 collective-permute-start.1
  18.3 7.3 collective-permute-start
  25.6 5.9 fusion.13
  31.5 0.8 fusion.9
  32.3 3.2 fusion.101
  35.5 1.7 fusion.6
  37.2 10.4 %all-to-all-start = ((bf16[16,16,1536]{2,1,0:T(8,128)(2,1)}), bf16[16,16,1536]{2,1,0:T(8,128)(2,1)S(1)}, u32[]{:S(2)}, u32[]{:S(2)}) async-start(bf16[16,16,1536]{2,1,0:T(8,128)(2,1)} %bitcast.190), calls=%async_computation | async-start | bytes 1572864 | tf_op jit(solution)/shard_map/all_to_all | solution.py:96
  47.8 2.0 copy.32
  51.0 6.4 scatter_custom_fusion
  57.8 18.2 %all-to-all-done = bf16[16,16,1536]{2,1,0:T(8,128)(2,1)S(1)} async-done(((bf16[16,16,1536]{2,1,0:T(8,128)(2,1)}), bf16[16,16,1536]{2,1,0:T(8,128)(2,1)S(1)}, u32[]{:S(2)}, u32[]{:S(2)}) %all-to-all-start) | async-done | bytes 786464 | tf_op jit(solution)/shard_map/all_to_all | solution.py:96
  76.0 0.9 rev.14
  77.0 4.0 all-to-all-start.1
  81.1 235.8 %all-gather.5.cloned.1.call-done = bf16[1536,4096]{1,0:T(8,128)(2,1)} async-done(((bf16[1536,256]{1,0:T(8,128)(2,1)}), bf16[1536,4096]{1,0:T(8,128)(2,1)}) %all-gather.5.cloned.1.call-update) | async-done | bytes 12582928 | tf_op jit(solution)/shard_map/all_gather | solution.py:74
  316.9 6.6 fusion.195
  323.6 1.9 copy-done.14
  325.5 3.2 convolution_convert_fusion
  329.0 1.2 copy.35
  330.1 10.3 %rev.15 = bf16[256,1536]{0,1:T(8,128)(2,1)S(1)} reverse(bf16[256,1536]{0,1:T(8,128)(2,1)} %copy.35), dimensions={0} | reverse | bytes 1572864 | tf_op jit(solution)/shard_map/rev | solution.py:99
  340.5 1.3 convert_element_type.86
  341.8 6.1 gather_fusion.1
  347.9 3.0 copy.37
  350.9 6.1 gather_fusion
  357.0 3.1 copy.36
  360.1 148.2 %all-reduce.3.cloned.1.call-done = bf16[64,4096]{1,0:T(8,128)(2,1)} async-done(((bf16[64,4096]{1,0:T(8,128)(2,1)}), bf16[64,4096]{1,0:T(8,128)(2,1)}) %all-reduce.3.cloned.1.call-update) | async-done | bytes 524304
  508.3 0.9 constant_dynamic-slice_fusion
  509.7 7.9 %rev.12 = f32[4,2048,2]{0,2,1:T(2,128)} reverse(bf16[4,2048,2]{0,2,1:T(2,128)(2,1)S(1)} %bitcast.184), dimensions={2} | reverse | bytes 98304 | tf_op jit(solution)/shard_map/rev | solution.py:30
  517.5 3.7 fusion.19
  521.2 10.3 %rev.13 = bf16[4,2048,2]{0,2,1:T(2,128)(2,1)} reverse(bf16[4,2048,2]{0,2,1:T(2,128)(2,1)} %bitcast.185), dimensions={2} | reverse | bytes 65536 | tf_op jit(solution)/shard_map/rev | solution.py:30
  531.4 2.3 select_bitcast_fusion
  533.8 1.6 copy.34
  535.4 31.2 %all-gather.1 = bf16[16,4,4096]{2,1,0:T(4,128)(2,1)S(1)} all-gather(bf16[1,4,4096]{2,1,0:T(4,128)(2,1)S(1)} %copy.34), channel_id=1, replica_groups=mesh['bins'=16,'batch'=16] {'bins'}, dimensions={0}, use_global_device_ids=true | all-gather | bytes 557056 | tf_op jit(solution)/shard_map/all_gather | solution.py:87
  566.6 0.9 reshape.132
  567.5 10.1 %fusion.5 = bf16[256,1536]{1,0:T(8,128)(2,1)S(1)} fusion(bf16[1536,4096]{1,0:T(8,128)(2,1)} %all-gather.5.cloned.1.call-done, bf16[64,4096]{1,0:T(8,128)(2,1)} %reshape.132, f32[256,4096]{1,0:T(8,128)} %copy-done.14, f32[1536,256]{0,1:T(8,128)} %copy.36, f32[1536,256]{0,1:T(8,128)} %copy.37, bf16[256,1536]{1,0:T(8,128)(2,1)} %fusion.6, ...), kind=kOutput, calls=%fused_computation.15 | convolution fusion | flops 3363045376 | bytes 22052864 | tf_op jit(solution)/shard_map/dot_general | solution.py:92
  577.5 2.2 convolution_convert_fusion.1
  580.1 77.4 %reduce-scatter.2.cloned.1.call-done = bf16[48,1536]{1,0:T(8,128)(2,1)} async-done(((bf16[768,1536]{1,0:T(8,128)(2,1)}), bf16[48,1536]{1,0:T(8,128)(2,1)}) %reduce-scatter.2.cloned.1.call-update) | async-done | bytes 147472 | tf_op jit(solution)/shard_map/reduce_scatter | solution.py:106
  657.5 2.0 fusion.98
  659.5 16.7 %collective-permute-start.3 = (bf16[16,768]{1,0:T(8,128)(2,1)S(1)}, bf16[16,768]{1,0:T(8,128)(2,1)S(1)}, u32[]{:S(2)}, u32[]{:S(2)}) collective-permute-start(bf16[16,768]{1,0:T(8,128)(2,1)S(1)} %get-tuple-element.5), channel_id=1, source_target_pairs={{0,16},{16,32},{32,48},{48,64},{64,80},{80,96},{96,112},{112,128},... | collective-permute-start | bytes 73736 | tf_op jit(solution)/shard_map/ppermute | solution.py:14
  676.2 2.5 fusion.11
  678.7 2.1 collective-permute-start.2
  680.8 2.5 fusion.7
  683.3 5.7 collective-permute-done.2
  689.0 3.1 fusion.56
  692.1 1.4 fusion.108
  693.5 39.4 %all-gather.7.cloned.1.call-done = bf16[768,1536]{1,0:T(8,128)(2,1)} async-done(((bf16[48,1536]{1,0:T(8,128)(2,1)}), bf16[768,1536]{1,0:T(8,128)(2,1)}) %all-gather.7.cloned.1.call-update) | async-done | bytes 2359312 | tf_op jit(solution)/shard_map/all_gather | solution.py:114
  732.9 2.0 reduce_sum.42
  734.9 0.7 convert_element_type.92
  (62 shorter events, 2.9 us)
Async XLA Ops:
  7.2 28.4 %copy-start = (bf16[768,1536]{1,0:T(8,128)(2,1)S(1)}, bf16[768,1536]{1,0:T(8,128)(2,1)}, u32[]{:S(2)}) copy-start(bf16[768,1536]{1,0:T(8,128)(2,1)} %param.13) | copy-start | bytes 7077892
  7.2 2.2 copy-start.2
  7.2 2.2 copy-start.8
  7.2 309.7 %all-gather.5.cloned.1.call-start = ((), (), s32[]{:S(2)}) async-start(), calls=%async_computation.3 | async-start | bytes 13369344 | tf_op jit(solution)/shard_map/all_gather | solution.py:74
  13.2 18.3 %collective-permute-start.1 = (bf16[16,1536]{1,0:T(8,128)(2,1)S(1)}, bf16[16,1536]{1,0:T(8,128)(2,1)S(1)}, u32[]{:S(2)}, u32[]{:S(2)}) collective-permute-start(bf16[16,1536]{1,0:T(8,128)(2,1)S(1)} %get-tuple-element.3), channel_id=1, source_target_pairs={{16,0},{32,16},{48,32},{64,48},{80,64},{96,80},{112,96},{128,112},... | collective-permute-start | bytes 147464 | tf_op jit(solution)/shard_map/ppermute | solution.py:17
  18.3 13.2 %slice-start = ((s8[7077888]{0:T(1024)(128)(4,1)}), s8[4194304]{0:T(1024)(128)(4,1)S(1)}, s32[]{:S(2)}) async-start(s8[7077888]{0:T(1024)(128)(4,1)} %bitcast.193), calls=%async_computation.7 | async-start | bytes 8388608
  18.3 13.2 %slice-start.1 = ((s8[7077888]{0:T(1024)(128)(4,1)}), s8[2883584]{0:T(1024)(128)(4,1)S(1)}, s32[]{:S(2)}) async-start(s8[7077888]{0:T(1024)(128)(4,1)} %bitcast.193), calls=%async_computation.8 | async-start | bytes 5767168
  18.3 14.0 %collective-permute-start = (bf16[16,1536]{1,0:T(8,128)(2,1)S(1)}, bf16[16,1536]{1,0:T(8,128)(2,1)S(1)}, u32[]{:S(2)}, u32[]{:S(2)}) collective-permute-start(bf16[16,1536]{1,0:T(8,128)(2,1)S(1)} %get-tuple-element.2), channel_id=1, source_target_pairs={{0,16},{16,32},{32,48},{48,64},{64,80},{80,96},{96,112},{112,128},... | collective-permute-start | bytes 147464 | tf_op jit(solution)/shard_map/ppermute | solution.py:14
  35.5 1.7 copy-start.4
  37.2 10.5 %copy-start.10 = (s32[1,64,8]{1,2,0:T(8,128)S(1)}, s32[1,64,8]{1,2,0:T(8,128)}, u32[]{:S(2)}) copy-start(s32[1,64,8]{1,2,0:T(8,128)} %param.16) | copy-start | bytes 6148
  37.2 10.6 %copy-start.6 = (f32[1,4,4096]{2,1,0:T(4,128)S(1)}, f32[1,4,4096]{2,1,0:T(4,128)}, u32[]{:S(2)}) copy-start(f32[1,4,4096]{2,1,0:T(4,128)} %param.19) | copy-start | bytes 196612
  37.2 12.6 %copy-start.13 = (u32[256]{0:T(256)S(1)}, u32[256]{0:T(256)}, u32[]{:S(2)}) copy-start(u32[256]{0:T(256)} %constant.22) | copy-start | bytes 3076
  37.2 13.8 %copy-start.9 = (s32[1536]{0:T(1024)S(1)}, s32[1536]{0:T(1024)}, u32[]{:S(2)}) copy-start(s32[1536]{0:T(1024)} %param.15) | copy-start | bytes 18436
  37.2 20.2 %copy-start.11 = (s32[1,64]{1,0:T(1,128)S(1)}, s32[1,64]{1,0:T(1,128)}, u32[]{:S(2)}) copy-start(s32[1,64]{1,0:T(1,128)} %param.17) | copy-start | bytes 772
  37.2 38.8 %all-to-all-start = ((bf16[16,16,1536]{2,1,0:T(8,128)(2,1)}), bf16[16,16,1536]{2,1,0:T(8,128)(2,1)S(1)}, u32[]{:S(2)}, u32[]{:S(2)}) async-start(bf16[16,16,1536]{2,1,0:T(8,128)(2,1)} %bitcast.190), calls=%async_computation | async-start | bytes 1572864 | tf_op jit(solution)/shard_map/all_to_all | solution.py:96
  57.8 265.8 %copy-start.7 = (bf16[64,256]{1,0:T(8,128)(2,1)}, bf16[64,256]{1,0:T(8,128)(2,1)S(1)}, u32[]{:S(2)}) copy-start(bf16[64,256]{1,0:T(8,128)(2,1)S(1)} %convert_reduce_fusion) | copy-start | bytes 98308
  77.0 252.0 %all-to-all-start.1 = ((bf16[16,16,1536]{2,1,0:T(8,128)(2,1)}), bf16[16,16,1536]{2,1,0:T(8,128)(2,1)S(1)}, u32[]{:S(2)}, u32[]{:S(2)}) async-start(bf16[16,16,1536]{2,1,0:T(8,128)(2,1)} %rev.14), calls=%async_computation.1 | async-start | bytes 1572864 | tf_op jit(solution)/shard_map/all_to_all | solution.py:97
  81.0 427.3 %all-reduce.3.cloned.1.call-start = ((), (), s32[]{:S(2)}) async-start(), calls=%async_computation.6 | async-start | bytes 1048576
  323.6 2.0 copy-start.14
  325.5 3.3 copy-start.12
  328.8 328.7 %reduce-scatter.2.cloned.1.call-start = ((), (), s32[]{:S(2)}) async-start(), calls=%async_computation.4 | async-start | bytes 2506752 | tf_op jit(solution)/shard_map/reduce_scatter | solution.py:106
  521.2 10.3 %copy-start.1 = (bf16[4,4096]{0,1:T(8,128)(2,1)S(1)}, bf16[4,4096]{0,1:T(8,128)(2,1)}, u32[]{:S(2)}) copy-start(bf16[4,4096]{0,1:T(8,128)(2,1)} %fusion.19) | copy-start | bytes 98308
  567.5 10.1 %copy-start.5 = (bf16[256,768]{1,0:T(8,128)(2,1)S(1)}, bf16[256,768]{1,0:T(8,128)(2,1)}, u32[]{:S(2)}) copy-start(bf16[256,768]{1,0:T(8,128)(2,1)} %copy-done.4) | copy-start | bytes 1179652
  579.8 153.1 %all-gather.7.cloned.1.call-start = ((), (), s32[]{:S(2)}) async-start(), calls=%async_computation.5 | async-start | bytes 2506752 | tf_op jit(solution)/shard_map/all_gather | solution.py:114
  659.5 21.2 %collective-permute-start.3 = (bf16[16,768]{1,0:T(8,128)(2,1)S(1)}, bf16[16,768]{1,0:T(8,128)(2,1)S(1)}, u32[]{:S(2)}, u32[]{:S(2)}) collective-permute-start(bf16[16,768]{1,0:T(8,128)(2,1)S(1)} %get-tuple-element.5), channel_id=1, source_target_pairs={{0,16},{16,32},{32,48},{48,64},{64,80},{80,96},{96,112},{112,128},... | collective-permute-start | bytes 73736 | tf_op jit(solution)/shard_map/ppermute | solution.py:14
  678.7 10.3 %copy-start.3 = (bf16[1,256,1536]{2,1,0:T(8,128)(2,1)S(1)}, bf16[1,256,1536]{2,1,0:T(8,128)(2,1)}, u32[]{:S(2)}) copy-start(bf16[1,256,1536]{2,1,0:T(8,128)(2,1)} %param.10) | copy-start | bytes 2359300
  678.7 10.3 %collective-permute-start.2 = (bf16[16,768]{1,0:T(8,128)(2,1)S(1)}, bf16[16,768]{1,0:T(8,128)(2,1)S(1)}, u32[]{:S(2)}, u32[]{:S(2)}) collective-permute-start(bf16[16,768]{1,0:T(8,128)(2,1)S(1)} %get-tuple-element.4), channel_id=1, source_target_pairs={{16,0},{32,16},{48,32},{64,48},{80,64},{96,80},{112,96},{128,112},... | collective-permute-start | bytes 73736 | tf_op jit(solution)/shard_map/ppermute | solution.py:17
Sparse Core Ops, SparseCore 0:
  9.7 307.1 all-gather.4
  328.9 179.3 all-reduce.2
  579.9 77.5 reduce-scatter.1
  660.0 72.8 all-gather.6
